TPU v7x, 128 devices: a whole 4x4x4 slice. The times are simulated.
128 devices in a mesh: dom: 128 (over x, y, z, core).
Axes of the slice: x: 4, y: 4, z: 4, core: 2. Of those that a mesh axis runs over, the one named last changes fastest.
Arguments:
- features: bfloat16 [524288, 128], P('dom'), may hold values from -6 to 6
- hubs: bfloat16 [8192, 128], P('dom'), may hold values from -6 to 6
- weight: bfloat16 [128, 128], replicated, may hold values from -0.5 to 0.5
- bias: float32 [128], replicated, may hold values from -3 to 3
- cotangent: bfloat16 [524288, 128], P('dom'), may hold values from -6 to 6
- tiles: bfloat16 [65536, 128, 128], P('dom'), may hold values from 0 to 0.049804688
- tile_blocks: int32 [65536, 2], P('dom'), may hold values from 0 to 95, as said below
- tile_count: int32 [128], P('dom'), may hold values from 96 to 512, as said below
- halo_send: int32 [128, 128, 32], P('dom'), may hold values from 0 to 4095
- replica_rows: int32 [128, 128, 32], P('dom'), may hold values from 0 to 63
Outputs:
- activations: bfloat16 [524288, 128], P('dom')
- saliency: float32 [524288, 128], P('dom')
- hub_saliency: float32 [8192, 128], P('dom')
Inputs may be any that keep to these rules, and one draw needn't show every extreme that they name: `tile_blocks`: the first 96 tile slots of each partition name every column block of its extended table once; the others name any row and column blocks. `tile_count`: some partition has all 512 slots live.
All inputs are finite; a program needn't handle non-finite values.
Results may differ from a plain program's by a relative error of at most 0.0054.
Values may be sent and summed in bfloat16 or wider, within the bound.
No kernel may reach another device: no remote copies, remote signals or barrier semaphores. Data moves between devices by JAX's collectives and lax.ppermute only.
A program may use at most 128 MiB of HBM per device.

v0:
```python
import jax
import jax.numpy as jnp
from jax import lax
from jax.sharding import PartitionSpec as P


def silu_slope(preact):
    sigmoid = jax.nn.sigmoid(preact)
    return sigmoid * (1.0 + preact * (1.0 - sigmoid))


def body(
    features, hubs, weight, bias, cotangent, tiles, tile_blocks, tile_count, halo_send, replica_rows
):
    own_rows = features.shape[0]
    feature_dim = features.shape[1]
    parties = lax.axis_size("dom")
    tile_size = tiles.shape[1]
    boundary = halo_send.shape[2]
    batch_size = 16
    send_index = halo_send.reshape(-1)
    outgoing = features[send_index]
    wanted = replica_rows.reshape(parties, -1)
    arrived_rows = lax.all_to_all(outgoing, "dom", split_axis=0, concat_axis=0, tiled=True)
    hub_table = lax.all_gather(hubs, "dom", axis=0, tiled=True)
    offsets = jnp.arange(parties, dtype=jnp.int32)[:, None] * hubs.shape[0]
    hub_index = (wanted + offsets).reshape(-1)
    replicas = hub_table[hub_index]
    ext_table = jnp.concatenate([features, arrived_rows, replicas], 0)
    ext_blocks = ext_table.shape[0] // tile_size
    table_blocks = ext_table.reshape(ext_blocks, tile_size, feature_dim)
    row_blocks = own_rows // tile_size
    tile_total = tile_count[0]
    rounds = (tile_total + batch_size - 1) // batch_size
    lanes = jnp.arange(batch_size, dtype=jnp.int32)

    def fetch(turn_index):
        offset = turn_index * batch_size
        values = lax.dynamic_slice_in_dim(tiles, offset, batch_size, 0)
        places = lax.dynamic_slice_in_dim(tile_blocks, offset, batch_size, 0)
        active = (offset + lanes < tile_total)[:, None, None]
        return (values, places, active)

    def forward_turn(turn_index, summed):
        values, places, active = fetch(turn_index)
        product = jnp.einsum(
            "tij,tjf->tif", values, table_blocks[places[:, 1]], preferred_element_type=jnp.float32
        )
        return summed.at[places[:, 0]].add(jnp.where(active, product, 0.0))

    summed = lax.fori_loop(
        jnp.int32(0),
        rounds,
        forward_turn,
        jnp.zeros((row_blocks, tile_size, feature_dim), jnp.float32),
    )
    aggregated = summed.reshape(own_rows, feature_dim).astype(jnp.bfloat16)
    preact = jnp.dot(aggregated, weight, preferred_element_type=jnp.float32) + bias
    activations = jax.nn.silu(preact).astype(jnp.bfloat16)
    upstream = (cotangent.astype(jnp.float32) * silu_slope(preact)).astype(jnp.bfloat16)
    back_rows = jnp.einsum(
        "vh,fh->vf", upstream, weight, preferred_element_type=jnp.float32
    ).astype(jnp.bfloat16)
    back_blocks = back_rows.reshape(row_blocks, tile_size, feature_dim)

    def backward_turn(turn_index, gathered):
        values, places, active = fetch(turn_index)
        spread = jnp.einsum(
            "tij,tif->tjf", values, back_blocks[places[:, 0]], preferred_element_type=jnp.float32
        )
        return gathered.at[places[:, 1]].add(jnp.where(active, spread, 0.0))

    ext_grad = lax.fori_loop(
        jnp.int32(0),
        rounds,
        backward_turn,
        jnp.zeros((ext_blocks, tile_size, feature_dim), jnp.float32),
    )
    ext_grad = ext_grad.reshape(ext_blocks * tile_size, feature_dim)
    halo_end = own_rows + parties * boundary
    halo_part = ext_grad[own_rows:halo_end]
    replica_grad = ext_grad[halo_end:]
    returned_all = lax.all_to_all(
        halo_part.astype(jnp.bfloat16), "dom", split_axis=0, concat_axis=0, tiled=True
    ).astype(halo_part.dtype)
    partial_hub = jax.ops.segment_sum(replica_grad, hub_index, num_segments=parties * hubs.shape[0])
    hub_saliency = lax.psum_scatter(partial_hub, "dom", scatter_dimension=0, tiled=True)
    saliency = ext_grad[:own_rows] + jax.ops.segment_sum(
        returned_all, send_index, num_segments=own_rows
    )
    return (activations, saliency, hub_saliency)


def solution(mesh):
    placed = (
        P("dom", None),
        P("dom", None),
        P(),
        P(),
        P("dom", None),
        P("dom", None, None),
        P("dom", None),
        P("dom"),
        P("dom", None, None),
        P("dom", None, None),
    )
    return jax.shard_map(
        body,
        mesh=mesh,
        in_specs=placed,
        out_specs=(P("dom", None), P("dom", None), P("dom", None)),
        check_vma=False,
    )
```

profile of v0, /device:TPU:0, one launch (start us, length us, event | category | flops | bytes accessed | tf_op | source)
XLA Modules:
  0.0 1258.0 jit_solution(18225973054344951650)
XLA Ops:
  8.9 15.7 %gather_fusion.2 = bf16[4096,128]{1,0:T(8,128)(2,1)} fusion(bf16[4096,128]{1,0:T(8,128)(2,1)} %param.14, s32[4096]{0:T(1024)S(1)} %broadcast_clamp_fusion.1), kind=kCustom, calls=%fused_computation.2 | custom fusion | bytes 2113536 | tf_op jit(solution)/shard_map/gather | solution.py:22
  24.6 11.2 all-to-all-start
  37.0 44.2 %all-gather.2.cloned.1.call-done = bf16[8192,128]{1,0:T(8,128)(2,1)} async-done(((bf16[64,128]{1,0:T(8,128)(2,1)}), bf16[8192,128]{1,0:T(8,128)(2,1)}) %all-gather.2.cloned.1.call-update) | async-done | bytes 2097168 | tf_op jit(solution)/shard_map/all_gather | solution.py:25
  81.2 12.9 %gather_fusion.3 = bf16[4096,128]{1,0:T(8,128)(2,1)S(1)} fusion(bf16[8192,128]{1,0:T(8,128)(2,1)} %all-gather.2.cloned.1.call-done, s32[4096]{0:T(1024)S(1)} %broadcast_clamp_fusion), kind=kCustom, calls=%fused_computation.3 | custom fusion | bytes 2113536 | tf_op jit(solution)/shard_map/gather | solution.py:28
  94.1 16.4 %pad_maximum_fusion = bf16[12288,128]{1,0:T(8,128)(2,1)} fusion(bf16[4096,128]{1,0:T(8,128)(2,1)S(1)} %gather_fusion.3, bf16[4096,128]{1,0:T(8,128)(2,1)S(1)} %bitcast.39, bf16[4096,128]{1,0:T(8,128)(2,1)S(1)} %copy-done.1), kind=kLoop, calls=%fused_computation.34 | loop fusion | flops 9437184 | bytes 6291456 | tf_op jit(solution)/shard_map/concatenate | solution.py:29
  112.1 71.6 %while.22 = (s32[]{:T(128)}, f32[32,128,128]{2,1,0:T(8,128)}, s32[]{:T(128)}, s32[512,2]{0,1:T(2,128)S(1)}, s32[]{:T(128)}, /*index=5*/bf16[512,128,128]{2,1,0:T...) while((s32[]{:T(128)}, f32[32,128,128]{2,1,0:T(8,128)}, ...), condition=%wide.region_2.3_spmd.clone, body=%wide.region_0.2_spmd.clone.sunk | while | flops 67634312 | bytes 6296459 | solution.py:51
  116.8 3.3 scatter_fusion
  124.7 3.3 scatter_fusion
  132.7 3.3 scatter_fusion
  140.6 3.4 scatter_fusion
  148.6 3.3 scatter_fusion
  156.6 3.3 scatter_fusion
  164.5 3.3 scatter_fusion
  172.5 3.3 scatter_fusion
  180.5 3.3 scatter_fusion
  188.2 3.5 broadcast_in_dim.41
  191.6 55.9 %while.23 = (s32[]{:T(128)}, f32[96,128,128]{2,1,0:T(8,128)}, s32[]{:T(128)}, s32[512,2]{0,1:T(2,128)S(1)}, s32[]{:T(128)}, /*index=5*/bf16[512,128,128]{2,1,0:T...) while((s32[]{:T(128)}, f32[96,128,128]{2,1,0:T(8,128)}, ...), condition=%wide.region_5.6_spmd.clone, body=%wide.region_3.5_spmd.clone.sunk | while | flops 67634312 | bytes 6296459 | solution.py:73
  194.5 3.4 scatter_fusion.1
  200.7 3.4 scatter_fusion.1
  206.9 3.5 scatter_fusion.1
  213.1 3.4 scatter_fusion.1
  219.4 3.4 scatter_fusion.1
  225.6 3.4 scatter_fusion.1
  231.9 3.4 scatter_fusion.1
  238.0 3.4 scatter_fusion.1
  244.2 3.4 scatter_fusion.1
  247.6 3.9 fusion.19
  251.5 24.9 %scatter_custom_fusion.3 = f32[8192,128]{1,0:T(8,128)} fusion(s32[4096]{0:T(1024)S(1)} %bitcast.45, f32[4096,128]{1,0:T(8,128)} %bitcast.41, f32[]{:T(128)} %constant.39.clone.1), kind=kCustom, calls=%fused_computation.38 | custom fusion | flops 524288 | bytes 4194816 | tf_op jit(solution)/shard_map/scatter-add | solution.py:86
  279.2 330.6 %all-to-all-start.1 = ((bf16[128,32,128]{2,1,0:T(8,128)(2,1)}), bf16[128,32,128]{2,1,0:T(8,128)(2,1)S(1)}, u32[]{:S(2)}, u32[]{:S(2)}) async-start(bf16[128,32,128]{2,1,0:T(8,128)(2,1)} %bitcast.9), calls=%async_computation.1 | async-start | bytes 2097152 | tf_op jit(solution)/shard_map/all_to_all | solution.py:83
  609.9 19.3 %all-to-all-done.1 = bf16[128,32,128]{2,1,0:T(8,128)(2,1)S(1)} async-done(((bf16[128,32,128]{2,1,0:T(8,128)(2,1)}), bf16[128,32,128]{2,1,0:T(8,128)(2,1)S(1)}, u32[]{:S(2)}, u32[]{:S(2)}) %all-to-all-start.1) | async-done | bytes 1048608 | tf_op jit(solution)/shard_map/all_to_all | solution.py:83
  629.2 23.2 %scatter_custom_fusion.2 = f32[4096,128]{1,0:T(8,128)S(1)} fusion(f32[4096,128]{1,0:T(8,128)S(1)} %bitcast.40, s32[4096]{0:T(1024)S(1)} %reshape.168, bf16[4096,128]{1,0:T(8,128)(2,1)S(1)} %bitcast.38), kind=kCustom, calls=%fused_computation.36 | custom fusion | flops 1048576 | bytes 3145728 | tf_op jit(solution)/shard_map/scatter-add | solution.py:88
  652.4 598.8 %reduce-scatter.2.cloned.1.call-done = f32[64,128]{1,0:T(8,128)} async-done(((f32[8192,128]{1,0:T(8,128)}), f32[64,128]{1,0:T(8,128)}) %reduce-scatter.2.cloned.1.call-update) | async-done | bytes 32784 | tf_op jit(solution)/shard_map/reduce_scatter | solution.py:87
  (144 shorter events, 77.6 us)
Async XLA Ops:
  7.2 178.3 %copy-start = (bf16[128,128]{1,0:T(8,128)(2,1)S(1)}, bf16[128,128]{1,0:T(8,128)(2,1)}, u32[]{:S(2)}) copy-start(bf16[128,128]{1,0:T(8,128)(2,1)} %param.16) | copy-start | bytes 98308
  7.2 74.0 %all-gather.2.cloned.1.call-start = ((), (), s32[]{:S(2)}) async-start(), calls=%async_computation.3 | async-start | bytes 2113536 | tf_op jit(solution)/shard_map/all_gather | solution.py:25
  24.6 12.1 copy-start.4
  24.6 69.5 %all-to-all-start = ((bf16[128,32,128]{2,1,0:T(8,128)(2,1)}), bf16[128,32,128]{2,1,0:T(8,128)(2,1)S(1)}, u32[]{:S(2)}, u32[]{:S(2)}) async-start(bf16[128,32,128]{2,1,0:T(8,128)(2,1)} %bitcast.2), calls=%async_computation | async-start | bytes 2097152 | tf_op jit(solution)/shard_map/all_to_all | solution.py:24
  35.8 1215.4 %reduce-scatter.2.cloned.1.call-start = ((), (), s32[]{:S(2)}) async-start(), calls=%async_computation.4 | async-start | bytes 4227072 | tf_op jit(solution)/shard_map/reduce_scatter | solution.py:87
  37.0 57.1 %copy-start.1 = (bf16[4096,128]{1,0:T(8,128)(2,1)S(1)}, bf16[4096,128]{1,0:T(8,128)(2,1)}, u32[]{:S(2)}) copy-start(bf16[4096,128]{1,0:T(8,128)(2,1)} %param.14) | copy-start | bytes 3145732
  110.5 1.6 copy-start.3
  183.7 1.8 copy-start.6
  185.5 1.7 copy-start.5
  279.2 350.0 %all-to-all-start.1 = ((bf16[128,32,128]{2,1,0:T(8,128)(2,1)}), bf16[128,32,128]{2,1,0:T(8,128)(2,1)S(1)}, u32[]{:S(2)}, u32[]{:S(2)}) async-start(bf16[128,32,128]{2,1,0:T(8,128)(2,1)} %bitcast.9), calls=%async_computation.1 | async-start | bytes 2097152 | tf_op jit(solution)/shard_map/all_to_all | solution.py:83
  652.3 598.8 %copy-start.2 = (f32[4096,128]{1,0:T(8,128)}, f32[4096,128]{1,0:T(8,128)S(1)}, u32[]{:S(2)}) copy-start(f32[4096,128]{1,0:T(8,128)S(1)} %scatter_custom_fusion.2) | copy-start | bytes 6291460
Sparse Core Ops, SparseCore 0:
  11.1 70.0 all-gather.1
  276.6 974.5 reduce-scatter.1
where the time goes:
time: 1270 us; the launch traced here: 1260 us
  waiting for transfers between devices  663 us (52%)
  starting transfers between devices  342 us (27%)
  other arithmetic  139 us (11%)
  local copies, waits for them, and re-layouts  71.7 us (6%)
  matrix products  27.3 us (2%)
  between operations  14.9 us (1%)
    reduce_scatter x1, waiting for transfers between devices, body(): lax.psum_scatter(partial_hub, 'dom', scatter_dimension=0, tiled=True)  599 us
    all_to_all x1, starting transfers between devices, body(): lax.all_to_all(halo_part.astype(jnp.bfloat16), 'dom', split_axis=0, conca...  331 us
    all_gather x1, waiting for transfers between devices, body(): hub_table = lax.all_gather(hubs, 'dom', axis=0, tiled=True)  44.2 us
    scatter-add x9, other arithmetic, backward_turn(): return gathered.at[places[:, 1]].add(jnp.where(active, spread, 0.0))  30.6 us
    scatter-add x9, other arithmetic, forward_turn(): return summed.at[places[:, 0]].add(jnp.where(active, product, 0.0))  29.8 us
  transfers between devices with their start and end apart: 4, of which 3 were waited for; matrix products, arithmetic and copies ran while one was open for 4% of the time, Pallas kernels for 0%

commit v1 on v0

v1 whole, which is shorter than its diff:
```python
import functools

import jax
import jax.numpy as jnp
from jax import lax
from jax.experimental import pallas as pl
from jax.experimental.pallas import tpu as pltpu
from jax.sharding import PartitionSpec as P

VMEM = pltpu.VMEM
SMEM = pltpu.SMEM
F32 = jnp.float32
BF16 = jnp.bfloat16
I32 = jnp.int32
UNROLL = 8
NT = (((1,), (1,)), ((), ()))


def whole(space):
    return pl.BlockSpec(memory_space=space)


def params(mib=None):
    return pltpu.CompilerParams(
        vmem_limit_bytes=None if mib is None else mib << 20
    )


def outgoing_kernel(send_ref, feat_ref, hub_ref, wanted_ref, out_ref, wide, stage):
    step = pl.program_id(0)
    parties = out_ref.shape[0]
    rows = send_ref.shape[1]
    half = hub_ref.shape[0] // 2

    @pl.when(step == 0)
    def _():
        wide[...] = feat_ref[...].astype(F32)

    halves = (hub_ref[:half, :], hub_ref[half:, :])
    repeat = feat_ref.shape[1] // wanted_ref.shape[1]

    @pl.loop(0, parties // 2)
    def _(pair):
        for side in range(2):
            q = pair * 2 + side
            for j in range(rows):
                row = send_ref[step * parties + q, j]
                stage[side, pl.ds(j, 1), :] = wide[pl.ds(row, 1), :]
            out_ref[q, 0:rows, :] = stage[side].astype(BF16)
            out_ref[q, rows : rows + half, :] = halves[side]
            names = wanted_ref[pl.ds(q, 1), :].astype(F32)
            names = jnp.concatenate([names] * repeat, axis=1)
            out_ref[q, rows + half :, :] = jnp.broadcast_to(
                names, (out_ref.shape[1] - rows - half, names.shape[1])
            ).astype(BF16)


def outgoing_rows(send, features, hubs, wanted):
    parties, rows = send.shape
    width = features.shape[1]
    half = hubs.shape[0] // 2
    total = rows + half + 8
    steps = 8
    chunk = parties // steps
    return pl.pallas_call(
        outgoing_kernel,
        name="outgoing_rows",
        grid=(steps,),
        in_specs=[
            whole(SMEM),
            pl.BlockSpec(features.shape, lambda i: (0, 0)),
            pl.BlockSpec(hubs.shape, lambda i: (0, 0)),
            pl.BlockSpec((chunk, wanted.shape[1]), lambda i: (i, 0)),
        ],
        out_specs=pl.BlockSpec((chunk, total, width), lambda i: (i, 0, 0)),
        out_shape=jax.ShapeDtypeStruct((parties, total, width), BF16),
        scratch_shapes=[VMEM(features.shape, F32), VMEM((2, rows, width), F32)],
        compiler_params=params(),
        cost_estimate=pl.CostEstimate(flops=0, bytes_accessed=30 << 20, transcendentals=0),
    )(send, features, hubs, wanted)


def unpack(entry):
    return entry & 1023, (entry >> 10) & 63, entry >> 16


def tile_loop(list_ref, kind, live, tiles_ref, ring, sems, body):
    depth = ring.shape[0]
    groups = (live + UNROLL - 1) // UNROLL

    def start(group):
        slot = group % depth
        for u in range(UNROLL):
            tile, _, _ = unpack(list_ref[kind, group * UNROLL + u])
            pltpu.make_async_copy(tiles_ref.at[tile], ring.at[slot, u], sems.at[slot]).start()

    for ahead in range(depth - 1):

        @pl.when(ahead < groups)
        def _():
            start(jnp.int32(ahead))

    @pl.loop(0, groups)
    def _(group):
        @pl.when(group + depth - 1 < groups)
        def _():
            start(group + depth - 1)

        slot = group % depth
        pltpu.make_async_copy(
            tiles_ref.at[pl.ds(0, UNROLL)], ring.at[slot], sems.at[slot]
        ).wait()
        for u in range(UNROLL):
            _, row, column = unpack(list_ref[kind, group * UNROLL + u])
            body(ring[slot, u], row, column)


def own_forward_kernel(count_ref, rows_ref, feat_ref, tiles_ref, sum_ref, list_ref, live_ref, ring, total, sems):
    blocks = feat_ref.shape[0]
    count = count_ref[0]
    total[...] = jnp.zeros_like(total)

    def classify(t, lives):
        row = rows_ref[t, 0]
        column = rows_ref[t, 1]
        kind = column // blocks
        entry = t | (row << 10) | (column << 16)
        place = jnp.where(kind == 0, lives[0], jnp.where(kind == 1, lives[1], lives[2]))
        list_ref[kind, place] = entry
        return tuple(lives[k] + (kind == k).astype(I32) for k in range(3))

    lives = lax.fori_loop(0, count, classify, (jnp.int32(0),) * 3)
    for k in range(3):
        live_ref[k] = lives[k]
        for u in range(UNROLL):
            list_ref[k, lives[k] + u] = jnp.int32((blocks << 10) | (3 * blocks << 16))

    def body(values, row, column):
        column = jnp.minimum(column, blocks - 1)
        total[row] += jnp.dot(values, feat_ref[column], preferred_element_type=F32)

    tile_loop(list_ref, 0, lives[0], tiles_ref, ring, sems, body)
    sum_ref[...] = total[:blocks]


def own_forward(count, places, features, tiles):
    tile = tiles.shape[1]
    blocks = features.shape[0] // tile
    width = features.shape[1]
    slots = tiles.shape[0] + UNROLL
    return pl.pallas_call(
        own_forward_kernel,
        name="own_forward",
        in_specs=[whole(SMEM), whole(SMEM), whole(VMEM), whole(pl.ANY)],
        out_specs=[whole(VMEM), whole(SMEM), whole(SMEM)],
        out_shape=[
            jax.ShapeDtypeStruct((blocks, tile, width), F32),
            jax.ShapeDtypeStruct((3, slots), I32),
            jax.ShapeDtypeStruct((3,), I32),
        ],
        scratch_shapes=[
            VMEM((4, UNROLL, tile, tile), BF16),
            VMEM((blocks + 1, tile, width), F32),
            pltpu.SemaphoreType.DMA((4,)),
        ],
        compiler_params=params(),
        cost_estimate=pl.CostEstimate(flops=10**9, bytes_accessed=40 << 20, transcendentals=0),
    )(count, places, features.reshape(blocks, tile, width), tiles)


def middle_kernel(
    list_ref, live_ref, side_ref, arrived_ref, other_ref, wanted_ref, start_ref, weight_ref, bias_ref,
    cot_ref, tiles_ref, act_ref, back_ref, grads_ref, ring, table, total, swapped, spread, sems,
):
    blocks, tile, width = start_ref.shape
    parties = arrived_ref.shape[0]
    rows = tile * blocks // parties
    group = tile // rows
    half = arrived_ref.shape[1] - rows - 8
    total[:blocks] = start_ref[...]
    weight = weight_ref[...]

    for b in range(blocks):
        table[b] = arrived_ref[b * group : (b + 1) * group, 0:rows, :].reshape(tile, width)

    def boundary_body(values, row, column):
        total[row] += jnp.dot(values, table[column - blocks], preferred_element_type=F32)

    tile_loop(list_ref, 1, live_ref[1], tiles_ref, ring, sems, boundary_body)

    side = side_ref[0]

    @pl.loop(0, blocks)
    def _(b):
        near = arrived_ref[pl.ds(b * group, group), rows : rows + half, :].reshape(group * half, width)
        far = other_ref[pl.ds(b * group, group), rows : rows + half, :].reshape(group * half, width)
        names = wanted_ref[b]
        lane = lax.broadcasted_iota(I32, (tile, group * half), 1)
        party = lax.broadcasted_iota(I32, (tile, group * half), 0) // rows
        is_far = ((names >= half).astype(I32) != side).astype(I32)
        target = jnp.where(names >= half, names - half, names) + party * half
        near_hot = jnp.where((lane == target) & (is_far == 0), 1.0, 0.0).astype(BF16)
        far_hot = jnp.where((lane == target) & (is_far == 1), 1.0, 0.0).astype(BF16)
        picked = jnp.dot(near_hot, near, preferred_element_type=F32)
        picked += jnp.dot(far_hot, far, preferred_element_type=F32)
        table[blocks + b] = picked.astype(BF16)

    tile_loop(list_ref, 2, live_ref[2], tiles_ref, ring, sems, boundary_body)

    @pl.loop(0, blocks)
    def _(b):
        preact = jnp.dot(total[b].astype(BF16), weight, preferred_element_type=F32) + bias_ref[...]
        sigmoid = 1.0 / (1.0 + jnp.exp(-preact))
        act_ref[b] = (preact * sigmoid).astype(BF16)
        slope = sigmoid * (1.0 + preact * (1.0 - sigmoid))
        upstream = (cot_ref[b].astype(F32) * slope).astype(BF16)
        swapped[b] = lax.dot_general(weight, upstream, NT, preferred_element_type=F32).astype(BF16)

    back_ref[...] = swapped[:blocks]
    spread[...] = jnp.zeros_like(spread)

    def backward_body(values, row, column):
        spread[column - blocks] += jnp.dot(swapped[row], values, preferred_element_type=F32)

    for kind in (1, 2):
        tile_loop(list_ref, kind, live_ref[kind], tiles_ref, ring, sems, backward_body)

    @pl.loop(0, blocks)
    def _(b):
        for part in range(2):
            out = jnp.transpose(spread[part * blocks + b]).astype(BF16)
            grads_ref[pl.ds(b * group, group), part * rows : (part + 1) * rows, :] = out.reshape(
                group, rows, width
            )


def middle(lists, lives, side, arrived, other, wanted, start, weight, bias, cotangent, tiles):
    blocks, tile, width = start.shape
    parties = arrived.shape[0]
    rows = tile * blocks // parties
    return pl.pallas_call(
        middle_kernel,
        name="middle",
        in_specs=[whole(SMEM)] * 3 + [whole(VMEM)] * 7 + [whole(pl.ANY)],
        out_specs=[whole(VMEM)] * 3,
        out_shape=[
            jax.ShapeDtypeStruct((blocks, tile, width), BF16),
            jax.ShapeDtypeStruct((blocks, width, tile), BF16),
            jax.ShapeDtypeStruct((parties, 2 * rows, width), BF16),
        ],
        scratch_shapes=[
            VMEM((4, UNROLL, tile, tile), BF16),
            VMEM((2 * blocks + 1, tile, width), BF16),
            VMEM((blocks + 1, tile, width), F32),
            VMEM((blocks + 1, width, tile), BF16),
            VMEM((2 * blocks + 1, width, tile), F32),
            pltpu.SemaphoreType.DMA((4,)),
        ],
        compiler_params=params(),
        cost_estimate=pl.CostEstimate(flops=4 * 10**9, bytes_accessed=60 << 20, transcendentals=10**6),
    )(
        lists, lives, side, arrived, other, wanted, start, weight, bias,
        cotangent.reshape(blocks, tile, width), tiles,
    )


def own_backward_kernel(list_ref, live_ref, back_ref, tiles_ref, own_ref, ring, swapped, spread, sems):
    blocks = back_ref.shape[0]
    swapped[:blocks] = back_ref[...]
    spread[...] = jnp.zeros_like(spread)

    def body(values, row, column):
        column = jnp.minimum(column, blocks)
        spread[column] += jnp.dot(swapped[row], values, preferred_element_type=F32)

    tile_loop(list_ref, 0, live_ref[0], tiles_ref, ring, sems, body)

    @pl.loop(0, blocks)
    def _(b):
        own_ref[b] = jnp.transpose(spread[b])


def own_backward(lists, lives, back, tiles):
    blocks, width, tile = back.shape
    return pl.pallas_call(
        own_backward_kernel,
        name="own_backward",
        in_specs=[whole(SMEM)] * 2 + [whole(VMEM), whole(pl.ANY)],
        out_specs=whole(VMEM),
        out_shape=jax.ShapeDtypeStruct((blocks, tile, width), F32),
        scratch_shapes=[
            VMEM((4, UNROLL, tile, tile), BF16),
            VMEM((blocks + 1, width, tile), BF16),
            VMEM((blocks + 1, width, tile), F32),
            pltpu.SemaphoreType.DMA((4,)),
        ],
        compiler_params=params(),
        cost_estimate=pl.CostEstimate(flops=10**9, bytes_accessed=40 << 20, transcendentals=0),
    )(lists, lives, back, tiles)


def returned_kernel(send_ref, own_ref, back_ref, names_ref, sal_ref, hub_ref, stage, chain1, chain2, chain3):
    parties, rows = send_ref.shape
    sal_ref[...] = own_ref[...]
    chains = (sal_ref, chain1, chain2, chain3)
    for chain in chains[1:]:
        chain[...] = jnp.zeros_like(chain)

    @pl.loop(0, parties)
    def _(q):
        stage[...] = back_ref[q, 0:rows, :].astype(F32)
        for j in range(rows):
            chain = chains[j % 4]
            row = send_ref[q, j]
            chain[pl.ds(row, 1), :] += stage[pl.ds(j, 1), :]

    sal_ref[...] += (chain1[...] + chain2[...]) + chain3[...]

    hubs, width = hub_ref.shape
    group = width // rows
    total = jnp.zeros((hubs, width), F32)
    lane = lax.broadcasted_iota(I32, (1, width), 1) // rows
    hub = lax.broadcasted_iota(I32, (hubs, width), 0).astype(F32)
    base = names_ref.shape[1] - 8
    for b in range(parties // group):
        names = jnp.zeros((1, width), F32)
        for i in range(group):
            row = names_ref[b * group + i, base : base + 1, :].astype(F32)
            names = jnp.where(lane == i, row, names)
        hot = jnp.where(hub == names, 1.0, 0.0).astype(BF16)
        grads = back_ref[b * group : (b + 1) * group, rows:, :].reshape(group * rows, width)
        total += jnp.dot(hot, grads, preferred_element_type=F32)
    hub_ref[...] = total


def returned_rows(send, own, returned, arrived, hubs):
    rows, width = own.shape
    return pl.pallas_call(
        returned_kernel,
        name="returned_rows",
        in_specs=[whole(SMEM)] + [whole(VMEM)] * 3,
        out_specs=[whole(VMEM)] * 2,
        out_shape=[
            jax.ShapeDtypeStruct((rows, width), F32),
            jax.ShapeDtypeStruct((hubs, width), F32),
        ],
        scratch_shapes=[VMEM((send.shape[1], width), F32)] + [VMEM((rows, width), F32)] * 3,
        compiler_params=params(),
        cost_estimate=pl.CostEstimate(flops=10**8, bytes_accessed=40 << 20, transcendentals=0),
    )(send, own, returned, arrived)


def body(
    features, hubs, weight, bias, cotangent, tiles, tile_blocks, tile_count, halo_send, replica_rows
):
    own_rows, width = features.shape
    tile = tiles.shape[1]
    blocks = own_rows // tile
    send = halo_send[0]
    wanted = replica_rows[0]
    parties = send.shape[0]
    side = (lax.axis_index("dom") % 2).astype(I32).reshape(1)

    outgoing = outgoing_rows(send, features, hubs, wanted)
    arrived = lax.all_to_all(outgoing, "dom", split_axis=0, concat_axis=0, tiled=True)
    other = lax.ppermute(arrived, "dom", [(i, i ^ 1) for i in range(parties)])
    start, lists, lives = own_forward(tile_count, tile_blocks, features, tiles)
    names = wanted.reshape(blocks, tile, 1)
    act, back, grads = middle(
        lists, lives, side, arrived, other, names, start, weight, bias.reshape(1, -1), cotangent, tiles
    )
    returned = lax.all_to_all(grads, "dom", split_axis=0, concat_axis=0, tiled=True)
    own = own_backward(lists, lives, back, tiles)
    saliency, hub_saliency = returned_rows(
        send, own.reshape(own_rows, width), returned, arrived, hubs.shape[0]
    )
    return act.reshape(own_rows, width), saliency, hub_saliency


def solution(mesh):
    placed = (
        P("dom", None),
        P("dom", None),
        P(),
        P(),
        P("dom", None),
        P("dom", None, None),
        P("dom", None),
        P("dom"),
        P("dom", None, None),
        P("dom", None, None),
    )
    return jax.shard_map(
        body,
        mesh=mesh,
        in_specs=placed,
        out_specs=(P("dom", None), P("dom", None), P("dom", None)),
        check_vma=False,
    )
```

time: 1270 us -> 196 us (0.15)
  waiting for transfers between devices: 663 us -> 22.9 us
  starting transfers between devices: 342 us -> 37.9 us
  other arithmetic: 139 us -> 0 us
  Pallas kernels: 0 us -> 76.5 us
  local copies, waits for them, and re-layouts: 71.7 us -> 8.68 us
  blocking collectives: 0 us -> 44.6 us
  matrix products: 27.3 us -> 0 us
  between operations: 14.9 us -> 1.35 us
    reduce_scatter x1 -> x0, waiting for transfers between devices: 599 us -> none  [body(): lax.psum_scatter(partial_hub, 'dom', scatter_dimension=0, tiled=True)]
    all_to_all x2 -> x1, starting transfers between devices: 342 us -> 37.9 us  [body(): lax.all_to_all(grads, 'dom', split_axis=0, concat_axis=0, tiled=True)]
    scatter-add x20 -> x0, other arithmetic: 109 us -> none  [the longest x9 30.6 us: backward_turn(): return gathered.at[places[:, 1]].add(jnp.where(active, spread, 0.0))]
    pallas_call x0 -> x5, Pallas kernels: none -> 76.5 us  [the longest x1 35 us: middle(): pl.pallas_call(middle_kernel, name='middle', in_specs=[whole(SMEM)] * 3 +...]
    gather x20 -> x0, local copies, waits for them, and re-layouts: 57.2 us -> none  [the longest x9 22.8 us: forward_turn(): table_blocks[places[:, 1]]]
    all_to_all x0 -> x1, blocking collectives: none -> 44.6 us  [body(): lax.all_to_all(outgoing, 'dom', split_axis=0, concat_axis=0, tiled=True)]
    all_gather x1 -> x0, waiting for transfers between devices: 44.2 us -> none  [body(): hub_table = lax.all_gather(hubs, 'dom', axis=0, tiled=True)]
    dot_general x20 -> x0, matrix products: 27.3 us -> none  [the longest x9 12.6 us: backward_turn(): jnp.einsum('tij,tif->tjf', values, back_blocks[places[:, 0]], preferred_e...]
  transfers between devices with their start and end apart: 4 -> 2, of which waited for: 3 -> 1; matrix products, arithmetic and copies ran while one was open for 4% -> 2% of each run, Pallas kernels for 0% -> 9%
where the time goes in v1:
time: 196 us; the launch traced here: 192 us
  Pallas kernels  76.5 us (39%)
  blocking collectives  44.6 us (23%)
  starting transfers between devices  37.9 us (19%)
  waiting for transfers between devices  22.9 us (12%)
  local copies, waits for them, and re-layouts  8.68 us (4%)
    all_to_all x1, blocking collectives, body(): lax.all_to_all(outgoing, 'dom', split_axis=0, concat_axis=0, tiled=True)  44.6 us
    all_to_all x1, starting transfers between devices, body(): lax.all_to_all(grads, 'dom', split_axis=0, concat_axis=0, tiled=True)  37.9 us
    pallas_call x1, Pallas kernels, middle(): pl.pallas_call(middle_kernel, name='middle', in_specs=[whole(SMEM)] * 3 +...  35 us
    all_to_all x1, waiting for transfers between devices, body(): lax.all_to_all(grads, 'dom', split_axis=0, concat_axis=0, tiled=True)  22.9 us
    pallas_call x1, Pallas kernels, returned_rows(): pl.pallas_call(returned_kernel, name='returned_rows', in_specs=[whole(SME...  11.7 us
    pallas_call x1, Pallas kernels, outgoing_rows(): pl.pallas_call(outgoing_kernel, name='outgoing_rows', grid=(steps,), in_s...  11.6 us
    pallas_call x1, Pallas kernels, own_forward(): pl.pallas_call(own_forward_kernel, name='own_forward', in_specs=[whole(SM...  10.5 us
    pallas_call x1, Pallas kernels, own_backward(): pl.pallas_call(own_backward_kernel, name='own_backward', in_specs=[whole(...  7.71 us
  transfers between devices with their start and end apart: 2, of which 1 were waited for; matrix products, arithmetic and copies ran while one was open for 2% of the time, Pallas kernels for 9%

profile of v1, /device:TPU:0, one launch (start us, length us, event | category | flops | bytes accessed | tf_op | source)
XLA Modules:
  0.0 191.9 jit_solution(900582959655267585)
XLA Ops:
  0.6 1.4 copy.19
  2.1 1.4 copy.18
  3.5 11.6 %outgoing_rows.1 = bf16[128,72,128]{2,1,0:T(8,128)(2,1)} custom-call(s32[128,32]{1,0:T(8,128)} %bitcast.11, bf16[4096,128]{1,0:T(8,128)(2,1)} %feat_ref.1, bf16[64,128]{1,0:T(8,128)(2,1)} %hub_ref.1, s32[128,32]{1,0:T(8,128)} %bitcast.13), custom_call_target="tpu_custom_call" | custom-call | bytes 31457280 | tf_op jit(solution)/shard_map/outgoing_rows/pallas_call | solution.py:65
  15.1 0.0 copy-start.2
  15.1 44.6 %all_to_all.10.arrived_ref.names_ref = bf16[128,72,128]{2,1,0:T(8,128)(2,1)S(1)} all-to-all(bf16[128,72,128]{2,1,0:T(8,128)(2,1)} %outgoing_rows.1), channel_id=1, replica_groups=mesh['dom'=128] {'dom'}, dimensions={0} | all-to-all | bytes 4718592 | tf_op jit(solution)/shard_map/all_to_all | solution.py:365
  59.7 0.0 copy-start
  59.7 0.0 copy-start.3
  59.7 0.0 collective-permute-start
  59.7 0.0 copy-done.2
  59.7 3.6 %reshape_squeeze.4.wanted_ref = s32[32,128,1]{2,1,0:T(8,128)} reshape(s32[1,128,32]{2,1,0:T(8,128)S(1)} %copy-done.2) | data formatting | bytes 32768 | tf_op jit(solution)/shard_map/reshape;squeeze | solution.py:368
  63.9 0.0 copy-done.3
  64.0 0.9 copy.17.rows_ref
  64.8 10.5 %own_forward.1 = (f32[32,128,128]{2,1,0:T(8,128)}, s32[3,520]{1,0:T(4,128)}, s32[3]{0:T(128)}) custom-call(s32[1]{0:T(128)S(6)} %copy.22.count_ref, s32[512,2]{1,0:T(8,128)} %copy.17.rows_ref, bf16[32,128,128]{2,1,0:T(8,128)(2,1)} %bitcast.9, bf16[512,128,128]{2,1,0:T(8,128)(2,1)} %tiles_ref.5), custom_call_target="tpu_custom_call" | custom-call | flops 1000000000 | bytes 41943040 | tf_op jit(solution)/shard_map/own_forward/pallas_call | solution.py:151
  75.3 0.0 copy-done
  75.4 0.0 collective-permute-done.other_ref
  75.4 35.0 %middle.1 = (bf16[32,128,128]{2,1,0:T(8,128)(2,1)}, bf16[32,128,128]{2,1,0:T(8,128)(2,1)}, bf16[128,64,128]{2,1,0:T(8,128)(2,1)}) custom-call(s32[3,520]{1,0:T(4,128)} %get-tuple-element.11.list_ref, s32[3]{0:T(128)} %get-tuple-element.12.live_ref, s32[1]{0:T(128)} %bitcast.1.side_ref, bf16[128,72,128]{2,1,0:T(8,128)(2,1)} %copy-done, ...), custom_call_target="tpu_custom_call" | custom-call | flops 4000000000 | bytes 62914560 | tf_op jit(solution)/shard_map/middle/pallas_call | solution.py:241
  110.4 37.9 %all-to-all-start.1 = ((bf16[128,64,128]{2,1,0:T(8,128)(2,1)}), bf16[128,64,128]{2,1,0:T(8,128)(2,1)S(1)}, u32[]{:S(2)}, u32[]{:S(2)}) async-start(bf16[128,64,128]{2,1,0:T(8,128)(2,1)} %get-tuple-element.16), calls=%async_computation.1 | async-start | bytes 4194304 | tf_op jit(solution)/shard_map/all_to_all | solution.py:372
  148.3 7.7 %own_backward.1 = f32[32,128,128]{2,1,0:T(8,128)} custom-call(s32[3,520]{1,0:T(4,128)} %get-tuple-element.11.list_ref, s32[3]{0:T(128)} %get-tuple-element.12.live_ref, bf16[32,128,128]{2,1,0:T(8,128)(2,1)} %get-tuple-element.15.back_ref, bf16[512,128,128]{2,1,0:T(8,128)(2,1)} %tiles_ref.5), custom_call_target="tpu_custom_call" | custom-call | flops 1000000000 | bytes 41943040 | tf_op jit(solution)/shard_map/own_backward/pallas_call | solution.py:285
  156.0 22.9 %all-to-all-done.1.back_ref = bf16[128,64,128]{2,1,0:T(8,128)(2,1)S(1)} async-done(((bf16[128,64,128]{2,1,0:T(8,128)(2,1)}), bf16[128,64,128]{2,1,0:T(8,128)(2,1)S(1)}, u32[]{:S(2)}, u32[]{:S(2)}) %all-to-all-start.1) | async-done | bytes 2097184 | tf_op jit(solution)/shard_map/all_to_all | solution.py:372
  178.9 0.0 copy-start.1
  178.9 1.3 copy-done.1
  180.2 11.7 %returned_rows.1 = (f32[4096,128]{1,0:T(8,128)}, f32[64,128]{1,0:T(8,128)}) custom-call(s32[128,32]{1,0:T(8,128)} %bitcast.12, f32[4096,128]{1,0:T(8,128)} %bitcast.8, bf16[128,64,128]{2,1,0:T(8,128)(2,1)} %copy-done.1, bf16[128,72,128]{2,1,0:T(8,128)(2,1)} %copy-done), custom_call_target="tpu_custom_call" | custom-call | flops 100000000 | bytes 41943040 | tf_op jit(solution)/shard_map/returned_rows/pallas_call | solution.py:338
Async XLA Ops:
  15.1 44.6 %copy-start.2 = (s32[1,128,32]{2,1,0:T(8,128)S(1)}, s32[1,128,32]{2,1,0:T(8,128)}, u32[]{:S(2)}) copy-start(s32[1,128,32]{2,1,0:T(8,128)} %copy.19) | copy-start | bytes 49156
  59.7 15.6 %copy-start = (bf16[128,72,128]{2,1,0:T(8,128)(2,1)}, bf16[128,72,128]{2,1,0:T(8,128)(2,1)S(1)}, u32[]{:S(2)}) copy-start(bf16[128,72,128]{2,1,0:T(8,128)(2,1)S(1)} %all_to_all.10.arrived_ref.names_ref) | copy-start | bytes 7077892
  59.7 4.2 %copy-start.3 = (s32[512,2]{0,1:T(2,128)S(1)}, s32[512,2]{0,1:T(2,128)}, u32[]{:S(2)}) copy-start(s32[512,2]{0,1:T(2,128)} %param.16) | copy-start | bytes 12292
  59.7 15.6 %collective-permute-start = (bf16[128,72,128]{2,1,0:T(8,128)(2,1)S(1)}, bf16[128,72,128]{2,1,0:T(8,128)(2,1)}, u32[]{:S(2)}, u32[]{:S(2)}) collective-permute-start(bf16[128,72,128]{2,1,0:T(8,128)(2,1)S(1)} %all_to_all.10.arrived_ref.names_ref), channel_id=1, source_target_pairs={{0,1},{1,0},{2,3},{3,2},{4,5},{5,4},{6,7},{7,6},{8,9},{9,8},{10,11... | collective-permute-start | bytes 7077896 | tf_op jit(solution)/shard_map/ppermute | solution.py:366
  110.4 68.5 %all-to-all-start.1 = ((bf16[128,64,128]{2,1,0:T(8,128)(2,1)}), bf16[128,64,128]{2,1,0:T(8,128)(2,1)S(1)}, u32[]{:S(2)}, u32[]{:S(2)}) async-start(bf16[128,64,128]{2,1,0:T(8,128)(2,1)} %get-tuple-element.16), calls=%async_computation.1 | async-start | bytes 4194304 | tf_op jit(solution)/shard_map/all_to_all | solution.py:372
  178.9 1.3 copy-start.1
